TPU v7x, 32 devices: a whole 2x2x4 slice. The times are simulated.
32 devices in a mesh: dp: 4 (over z), vocab: 8 (over y, x, core).
Axes of the slice: x: 2, y: 2, z: 4, core: 2. Of those that a mesh axis runs over, the one named last changes fastest.
Arguments:
- hidden: bfloat16 [4096, 4096], P(('dp', 'vocab')), may hold values from -4 to 4
- output_weight: bfloat16 [4096, 8192], P(None, 'vocab'), may hold values from -0.09375 to 0.09375
- owners: int32 [4096, 3], P(('dp', 'vocab')), may hold values from 0 to 7, all different within a row; in each aligned block of 128 rows (0 to 127, 128 to 255, ...) at most 64 rows name the same one
- negatives: int32 [4096, 3, 2], P(('dp', 'vocab')), may hold values from 0 to 7
- negative_mask: int32 [4096, 3, 2], P(('dp', 'vocab')), may hold values 0 or 1
- target_block: int32 [4096], P(('dp', 'vocab')), may hold values from 0 to 7
- target_word: int32 [4096], P(('dp', 'vocab')), may hold values from 0 to 127
- log_norm: bfloat16 [4096], P(('dp', 'vocab')), may hold values from 1 to 2
- cotangent: bfloat16 [4096], P(('dp', 'vocab')), may hold values from 4 to 8
Outputs:
- hidden_grad: bfloat16 [4096, 4096], P(('dp', 'vocab'))
- weight_grad: bfloat16 [4096, 8192], P('dp', 'vocab')
Inputs may be any that keep to these rules, and one draw needn't show every extreme that they name: Each row names 3 different owners; among the 128 rows of one device no owner is named by more than 64 rows, and in some device's rows an owner is named by exactly 64.
All inputs are finite; a program needn't handle non-finite values. No bound on the sum of `negative_mask` on one device may be relied on, other than what follows from the above.
Results may differ from a plain program's by a relative error of at most 0.015.
Values may be sent and summed in bfloat16 or wider, within the bound.
A program may use at most 128 MiB of HBM per device.

v0:
```python
import jax
import jax.numpy as jnp
from jax import lax
from jax.sharding import PartitionSpec as P

BLOCK = 128
BLK_DEV = 8


def body(
    hidden,
    output_weight,
    owners,
    negatives,
    negative_mask,
    target_block,
    target_word,
    log_norm,
    cotangent,
):
    token_total, model_width = hidden.shape
    visits = owners.shape[1]
    owner_count = lax.axis_size("vocab")
    owner_words = output_weight.shape[1]
    capacity = max(2, token_total * visits * 4 // (3 * owner_count))
    entries = token_total * visits
    slot_total = owner_count * capacity
    flat_owner = owners.reshape(entries)
    owner_hot = (flat_owner[:, None] == jnp.arange(owner_count, dtype=jnp.int32)[None, :]).astype(
        jnp.int32
    )
    earlier = jnp.cumsum(owner_hot, axis=0) - owner_hot
    position = jnp.sum(earlier * owner_hot, axis=1)
    slot_index = flat_owner * capacity + position
    entry_ids = jnp.arange(entries, dtype=jnp.int32)
    token_of = entry_ids // visits
    is_first = entry_ids % visits == 0
    cluster_ids = jnp.arange(BLK_DEV, dtype=jnp.int32)
    negative_flat = negatives.reshape(entries, -1)
    mask_flat = negative_mask.reshape(entries, -1)
    target_here = jnp.where(is_first, target_block[token_of], -1)
    matched = (negative_flat[:, :, None] == cluster_ids[None, None, :]) & (
        mask_flat[:, :, None] == 1
    )
    cluster_counts = jnp.sum(jnp.where(matched, 1.0, 0.0), axis=1) + jnp.where(
        target_here[:, None] == cluster_ids[None, :], 1.0, 0.0
    )
    scalars = jnp.stack(
        [
            cotangent[token_of].astype(jnp.float32),
            log_norm[token_of].astype(jnp.float32),
            target_here.astype(jnp.float32),
            target_word[token_of].astype(jnp.float32),
        ],
        axis=1,
    )
    row_meta = jnp.concatenate([cluster_counts, scalars], axis=1).astype(jnp.bfloat16)
    send_meta = (
        jnp.zeros((slot_total, row_meta.shape[1]), jnp.bfloat16)
        .at[slot_index]
        .set(row_meta)
        .reshape(owner_count, capacity, -1)
    )
    send_rows = (
        jnp.zeros((slot_total, model_width), jnp.bfloat16)
        .at[slot_index]
        .set(hidden[token_of])
        .reshape(owner_count, capacity, model_width)
    )
    got_rows, got_meta = (
        lax.all_to_all(send_rows, "vocab", split_axis=0, concat_axis=0, tiled=True),
        lax.all_to_all(send_meta, "vocab", split_axis=0, concat_axis=0, tiled=True),
    )
    arrived_rows = got_rows.reshape(slot_total, model_width)
    arrived_meta = got_meta.reshape(slot_total, -1).astype(jnp.float32)
    scores = jnp.dot(arrived_rows, output_weight, preferred_element_type=jnp.float32)
    word_counts = jnp.broadcast_to(
        arrived_meta[:, :BLK_DEV, None], (slot_total, BLK_DEV, BLOCK)
    ).reshape(slot_total, owner_words)
    token_weight = arrived_meta[:, BLK_DEV]
    log_total = arrived_meta[:, BLK_DEV + 1]
    target_col = arrived_meta[:, BLK_DEV + 2] * BLOCK + arrived_meta[:, BLK_DEV + 3]
    word_position = jnp.arange(owner_words).astype(jnp.float32)
    target_hot = jnp.where(word_position[None, :] == target_col[:, None], 1.0, 0.0)
    score_grad = (
        token_weight[:, None] * (word_counts * jnp.exp(scores - log_total[:, None]) - target_hot)
    ).astype(jnp.bfloat16)
    grad_rows = lax.dot_general(
        score_grad, output_weight, (((1,), (1,)), ((), ())), preferred_element_type=jnp.float32
    )
    grad_rows = grad_rows.astype(jnp.bfloat16).reshape(owner_count, capacity, model_width)
    returned = lax.all_to_all(grad_rows, "vocab", split_axis=0, concat_axis=0, tiled=True)
    per_entry = returned.reshape(slot_total, model_width)[slot_index].astype(jnp.float32)
    hidden_grad = jnp.sum(per_entry.reshape(token_total, visits, model_width), axis=1).astype(
        jnp.bfloat16
    )
    weight_grad = lax.psum_scatter(
        lax.dot_general(
            arrived_rows, score_grad, (((0,), (0,)), ((), ())), preferred_element_type=jnp.float32
        ).astype(jnp.bfloat16),
        "dp",
        scatter_dimension=0,
        tiled=True,
    )
    return (hidden_grad, weight_grad)


def solution(mesh):
    placed = (
        P(("dp", "vocab"), None),
        P(None, "vocab"),
        P(("dp", "vocab"), None),
        P(("dp", "vocab"), None, None),
        P(("dp", "vocab"), None, None),
        P(("dp", "vocab")),
        P(("dp", "vocab")),
        P(("dp", "vocab")),
        P(("dp", "vocab")),
    )
    return jax.shard_map(
        body,
        mesh=mesh,
        in_specs=placed,
        out_specs=(P(("dp", "vocab"), None), P("dp", "vocab")),
        check_vma=False,
    )
```

profile of v0, /device:TPU:0, one launch (start us, length us, event | category | flops | bytes accessed | tf_op | source)
XLA Modules:
  0.0 273.6 jit_solution(14708446456167880455)
XLA Ops:
  7.3 3.5 %gather_fusion = s32[384]{0:T(512)S(1)} fusion(s32[128]{0:T(128)} %param.14, s32[1024]{0:T(1024)S(1)} %pad_clamp_fusion.1), kind=kCustom, calls=%fused_computation | custom fusion | bytes 4608 | tf_op jit(solution)/shard_map/gather | solution.py:41
  10.8 0.8 copy.63
  12.7 0.8 copy.65
  13.7 0.7 broadcast_compare_fusion
  14.8 2.7 gather_fusion.3
  17.6 2.7 gather_fusion.1
  20.3 2.7 gather_fusion.2
  23.3 0.9 reduce-window.6
  24.8 1.5 scatter_custom_fusion
  26.5 0.7 reshape.271
  27.2 5.4 %all-to-all-start = ((bf16[8,2,384]{2,1,0:T(2,128)(2,1)}), bf16[8,2,384]{2,1,0:T(2,128)(2,1)S(1)}, u32[]{:S(2)}, u32[]{:S(2)}) async-start(bf16[8,2,384]{2,1,0:T(2,128)(2,1)} %reshape.271), calls=%async_computation | async-start | bytes 24576 | tf_op jit(solution)/shard_map/all_to_all | solution.py:72
  32.6 16.6 %scatter_custom_fusion.1 = bf16[512,4096]{1,0:T(8,128)(2,1)} fusion(s32[384]{0:T(512)S(1)} %fusion.33, bf16[128,4096]{1,0:T(8,128)(2,1)S(1)} %copy-done, s32[1024]{0:T(1024)S(1)} %pad_clamp_fusion.1, bf16[]{:T(256)} %constant.15.clone.1), kind=kCustom, calls=%fused_computation.10 | custom fusion | bytes 4194306 | tf_op jit(solution)/shard_map/scatter | solution.py:67
  49.2 4.6 %all-to-all-start.1 = ((bf16[8,64,4096]{2,1,0:T(8,128)(2,1)}), bf16[8,64,4096]{2,1,0:T(8,128)(2,1)}, u32[]{:S(2)}, u32[]{:S(2)}) async-start(bf16[8,64,4096]{2,1,0:T(8,128)(2,1)} %bitcast.40), calls=%async_computation.1 | async-start | bytes 8388608 | tf_op jit(solution)/shard_map/all_to_all | solution.py:71
  54.2 48.7 %all-to-all-done.1 = bf16[8,64,4096]{2,1,0:T(8,128)(2,1)} async-done(((bf16[8,64,4096]{2,1,0:T(8,128)(2,1)}), bf16[8,64,4096]{2,1,0:T(8,128)(2,1)}, u32[]{:S(2)}, u32[]{:S(2)}) %all-to-all-start.1) | async-done | bytes 4194336 | tf_op jit(solution)/shard_map/all_to_all | solution.py:71
  102.9 8.1 %fusion.39 = f32[512,1024]{1,0:T(8,128)S(1)} fusion(bf16[512,4096]{1,0:T(8,128)(2,1)} %bitcast.5, bf16[4096,1024]{1,0:T(8,128)(2,1)} %param.10), kind=kOutput, calls=%fused_computation.76 | convolution fusion | flops 4294967296 | bytes 14680064 | tf_op jit(solution)/shard_map/dot_general | solution.py:76
  111.7 0.7 copy-done.4
  112.4 9.7 %convolution_convert_fusion = bf16[4096,1024]{1,0:T(8,128)(2,1)} fusion(bf16[512,4096]{1,0:T(8,128)(2,1)} %bitcast.5, f32[64,8,8,128]{3,2,1,0:T(8,128)S(1)} %bitcast.42, f32[512,1024]{1,0:T(8,128)S(1)} %fusion.39, f32[1024]{0:T(1024)S(1)} %iota_convert_fusion, f32[512]{0:T(512)S(1)} %bitcast.50, f32[512]{0:T(512)S(1)} %bitcast.52, f32[512]{0:T(512)S(1)} %bitcast.48), kind=kOutput, calls=%fused_computation.8 | convolution fusion | flops 4302831616 | bytes 16787456 | tf_op jit(solution)/shard_map/dot_general | solution.py:98
  122.1 10.9 %convolution_convert_fusion.1 = bf16[512,4096]{1,0:T(8,128)(2,1)} fusion(bf16[4096,1024]{1,0:T(8,128)(2,1)} %param.10, f32[64,8,8,128]{3,2,1,0:T(8,128)S(1)} %bitcast.43, f32[512,1024]{1,0:T(8,128)} %copy-done.4, f32[1024]{0:T(1024)S(1)} %iota_convert_fusion, f32[512]{0:T(512)S(1)} %bitcast.51, f32[512]{0:T(512)S(1)} %bitcast.53, f32[512]{0:T(512)S(1)} %bitcast.49), kind=kOutput, calls=%fused_computation.9 | convolution fusion | flops 4300734464 | bytes 16787456 | tf_op jit(solution)/shard_map/dot_general | solution.py:88
  133.0 4.9 %all-to-all-start.2 = ((bf16[8,64,4096]{2,1,0:T(8,128)(2,1)}), bf16[8,64,4096]{2,1,0:T(8,128)(2,1)}, u32[]{:S(2)}, u32[]{:S(2)}) async-start(bf16[8,64,4096]{2,1,0:T(8,128)(2,1)} %bitcast.41), calls=%async_computation.2 | async-start | bytes 8388608 | tf_op jit(solution)/shard_map/all_to_all | solution.py:92
  137.9 49.1 %all-to-all-done.2 = bf16[8,64,4096]{2,1,0:T(8,128)(2,1)} async-done(((bf16[8,64,4096]{2,1,0:T(8,128)(2,1)}), bf16[8,64,4096]{2,1,0:T(8,128)(2,1)}, u32[]{:S(2)}, u32[]{:S(2)}) %all-to-all-start.2) | async-done | bytes 4194336 | tf_op jit(solution)/shard_map/all_to_all | solution.py:92
  187.0 11.1 %gather_fusion.4 = bf16[384,4096]{1,0:T(8,128)(2,1)} fusion(bf16[512,4096]{1,0:T(8,128)(2,1)} %bitcast.9, s32[1024]{0:T(1024)S(1)} %pad_clamp_fusion), kind=kCustom, calls=%fused_computation.5 | custom fusion | bytes 6292992 | tf_op jit(solution)/shard_map/gather | solution.py:93
  198.1 7.2 %gather.29 = bf16[128,3,4096]{2,1,0:T(4,128)(2,1)} reshape(bf16[384,4096]{1,0:T(8,128)(2,1)} %gather_fusion.4) | data formatting | bytes 6291456 | tf_op jit(solution)/shard_map/gather | solution.py:93
  205.3 8.5 %reduce_sum.35 = bf16[128,4096]{1,0:T(8,128)(2,1)} reduce(bf16[128,3,4096]{2,1,0:T(4,128)(2,1)} %gather.29, bf16[]{:T(256)} %constant.15.clone.1), dimensions={1}, to_apply=%region_6.7 | reduce | flops 1048576 | bytes 4194306 | tf_op jit(solution)/shard_map/reduce_sum | solution.py:94
  213.8 52.5 %reduce-scatter.2.cloned.1.call-done = bf16[1024,1024]{1,0:T(8,128)(2,1)} async-done(((bf16[4096,1024]{1,0:T(8,128)(2,1)}), bf16[1024,1024]{1,0:T(8,128)(2,1)}) %reduce-scatter.2.cloned.1.call-update) | async-done | bytes 2097168 | tf_op jit(solution)/shard_map/reduce_scatter | solution.py:97
  (47 shorter events, 3.9 us)
Async XLA Ops:
  7.2 25.4 %copy-start = (bf16[128,4096]{1,0:T(8,128)(2,1)S(1)}, bf16[128,4096]{1,0:T(8,128)(2,1)}, u32[]{:S(2)}) copy-start(bf16[128,4096]{1,0:T(8,128)(2,1)} %param.9) | copy-start | bytes 3145732
  7.2 7.7 %copy-start.1 = (s32[128]{0:T(128)S(1)}, s32[128]{0:T(128)}, u32[]{:S(2)}) copy-start(s32[128]{0:T(128)} %param.15) | copy-start | bytes 1540
  7.2 10.4 %copy-start.2 = (bf16[128]{0:T(256)(128)(2,1)S(1)}, bf16[128]{0:T(256)(128)(2,1)}, u32[]{:S(2)}) copy-start(bf16[128]{0:T(256)(128)(2,1)} %param.17) | copy-start | bytes 772
  7.2 13.1 %copy-start.3 = (bf16[128]{0:T(256)(128)(2,1)S(1)}, bf16[128]{0:T(256)(128)(2,1)}, u32[]{:S(2)}) copy-start(bf16[128]{0:T(256)(128)(2,1)} %param.16) | copy-start | bytes 772
  27.2 22.1 %all-to-all-start = ((bf16[8,2,384]{2,1,0:T(2,128)(2,1)}), bf16[8,2,384]{2,1,0:T(2,128)(2,1)S(1)}, u32[]{:S(2)}, u32[]{:S(2)}) async-start(bf16[8,2,384]{2,1,0:T(2,128)(2,1)} %reshape.271), calls=%async_computation | async-start | bytes 24576 | tf_op jit(solution)/shard_map/all_to_all | solution.py:72
  49.2 53.7 %all-to-all-start.1 = ((bf16[8,64,4096]{2,1,0:T(8,128)(2,1)}), bf16[8,64,4096]{2,1,0:T(8,128)(2,1)}, u32[]{:S(2)}, u32[]{:S(2)}) async-start(bf16[8,64,4096]{2,1,0:T(8,128)(2,1)} %bitcast.40), calls=%async_computation.1 | async-start | bytes 8388608 | tf_op jit(solution)/shard_map/all_to_all | solution.py:71
  53.8 212.5 %reduce-scatter.2.cloned.1.call-start = ((), (), s32[]{:S(2)}) async-start(), calls=%async_computation.4 | async-start | bytes 10485760 | tf_op jit(solution)/shard_map/reduce_scatter | solution.py:97
  111.1 1.4 copy-start.4
  133.0 54.0 %all-to-all-start.2 = ((bf16[8,64,4096]{2,1,0:T(8,128)(2,1)}), bf16[8,64,4096]{2,1,0:T(8,128)(2,1)}, u32[]{:S(2)}, u32[]{:S(2)}) async-start(bf16[8,64,4096]{2,1,0:T(8,128)(2,1)} %bitcast.41), calls=%async_computation.2 | async-start | bytes 8388608 | tf_op jit(solution)/shard_map/all_to_all | solution.py:92
Sparse Core Ops, SparseCore 0:
  122.2 144.0 reduce-scatter.1
where the time goes:
time: 278 us; the launch traced here: 274 us
  waiting for transfers between devices  150 us (54%)
  local copies, waits for them, and re-layouts  53.9 us (19%)
  matrix products  28.7 us (10%)
  starting transfers between devices  14.9 us (5%)
  between operations  14.7 us (5%)
  other arithmetic  11 us (4%)
    reduce_scatter x1, waiting for transfers between devices, body(): lax.psum_scatter(lax.dot_general(arrived_rows, score_grad, (((0,), (0,)),...  52.5 us
    all_to_all x1, waiting for transfers between devices, body(): lax.all_to_all(grad_rows, 'vocab', split_axis=0, concat_axis=0, tiled=True)  49.1 us
    all_to_all x1, waiting for transfers between devices, body(): lax.all_to_all(send_rows, 'vocab', split_axis=0, concat_axis=0, tiled=True)  48.7 us
    gather x2, local copies, waits for them, and re-layouts, body(): returned.reshape(slot_total, model_width)[slot_index].astype(jnp.float32)  18.3 us
    scatter x1, local copies, waits for them, and re-layouts, body(): send_rows = jnp.zeros((slot_total, model_width), jnp.bfloat16).at[slot_in...  16.6 us
    dot_general x1, matrix products, body(): lax.dot_general(score_grad, output_weight, (((1,), (1,)), ((), ())), pref...  10.9 us
    dot_general x1, matrix products, body(): lax.dot_general(arrived_rows, score_grad, (((0,), (0,)), ((), ())), prefe...  9.65 us
    reduce_sum x1, other arithmetic, body(): jnp.sum(per_entry.reshape(token_total, visits, model_width), axis=1)  8.52 us
  transfers between devices with their start and end apart: 4, of which 3 were waited for; matrix products, arithmetic and copies ran while one was open for 20% of the time, Pallas kernels for 0%

commit v1 on v0

v1 whole, which is shorter than its diff:
```python
import jax
import jax.numpy as jnp
from jax import lax
from jax.sharding import PartitionSpec as P

BLOCK = 128
BLK_DEV = 8
F32 = jnp.float32
BF16 = jnp.bfloat16


def body(
    hidden,
    output_weight,
    owners,
    negatives,
    negative_mask,
    target_block,
    target_word,
    log_norm,
    cotangent,
):
    tokens, width = hidden.shape
    visits = owners.shape[1]
    per_own = negatives.shape[2]
    n_vocab = lax.axis_size("vocab")
    n_dp = lax.axis_size("dp")
    me = lax.axis_index("vocab")
    my_dp = lax.axis_index("dp")
    words = output_weight.shape[1]
    capacity = max(2, tokens * visits * 4 // (3 * n_vocab))
    slots = n_vocab * capacity
    part = width // n_dp

    facts = jnp.concatenate(
        [
            owners.T,
            negatives.reshape(tokens, -1).T,
            negative_mask.reshape(tokens, -1).T,
            target_block[None, :],
            target_word[None, :],
        ],
        axis=0,
    ).astype(BF16)
    facts = jnp.concatenate([facts, log_norm[None, :], cotangent[None, :]], axis=0)
    facts = lax.all_gather(facts, ("dp", "vocab"), axis=0, tiled=False)
    blocks = n_dp * n_vocab

    group_rows = lax.all_gather(hidden, "vocab", axis=0, tiled=False)
    part_rows = lax.all_to_all(hidden, "dp", split_axis=1, concat_axis=0, tiled=True)
    part_rows = lax.all_gather(part_rows.reshape(n_dp, tokens, part), "vocab", axis=1)

    f = facts.astype(F32)
    pairs = visits * per_own
    hit = f[:, :visits, :] == me.astype(F32)
    neg = f[:, visits : visits + pairs, :]
    mask = f[:, visits + pairs : visits + 2 * pairs, :]
    base = visits + 2 * pairs
    t_block, t_word, norm, cot = (f[:, base + i, :] for i in range(4))
    named = jnp.any(hit, axis=1)
    cand = [jnp.where(hit[:, 0], t_block + 1.0, 0.0)]
    for n in range(per_own):
        value = jnp.zeros_like(t_block)
        for v in range(visits):
            i = v * per_own + n
            value = jnp.where(hit[:, v] & (mask[:, i] == 1.0), neg[:, i] + 1.0, value)
        cand.append(value)
    only = []
    for k, value in enumerate(cand):
        for earlier in cand[:k]:
            value = jnp.where(value == earlier, 0.0, value)
        only.append(value)
    upper = jnp.triu(jnp.ones((tokens, tokens), BF16), 1)
    rank = jnp.dot(named.astype(BF16), upper, preferred_element_type=F32)
    place = jnp.where(named, rank, -1.0)
    pick = (
        place[:, None, :] == jnp.arange(capacity, dtype=jnp.int32).astype(F32)[None, :, None]
    ).astype(BF16)
    attrs = jnp.stack(cand + only + [t_word, norm, cot], axis=1).astype(BF16)
    slot_facts = jnp.einsum("sct,sat->sca", pick, attrs, preferred_element_type=F32)
    kinds = per_own + 1
    all_only = slot_facts[:, :, kinds : 2 * kinds].reshape(n_dp * slots, kinds)
    mine = lax.dynamic_slice_in_dim(slot_facts, my_dp * n_vocab, n_vocab, 0).reshape(slots, -1)
    my_pick = lax.dynamic_slice_in_dim(pick, my_dp * n_vocab, n_vocab, 0)

    rows = jnp.einsum("sct,sth->sch", my_pick, group_rows, preferred_element_type=F32)
    rows = rows.astype(BF16).reshape(slots, width)
    scores = jnp.dot(rows, output_weight, preferred_element_type=F32)
    word_ids = jnp.arange(words, dtype=jnp.int32)[None, :]
    word_block = (word_ids // BLOCK + 1).astype(F32)
    word_in = (word_ids % BLOCK).astype(F32)
    counts = jnp.zeros((slots, words), F32)
    for k in range(kinds):
        counts = counts + jnp.where(mine[:, k : k + 1] == word_block, 1.0, 0.0)
    hot = jnp.where(
        (mine[:, 0:1] == word_block) & (mine[:, 2 * kinds : 2 * kinds + 1] == word_in), 1.0, 0.0
    )
    norm_col = mine[:, 2 * kinds + 1 : 2 * kinds + 2]
    cot_col = mine[:, 2 * kinds + 2 : 2 * kinds + 3]
    grown = jnp.where(counts > 0.0, counts * jnp.exp(scores - norm_col), 0.0)
    grad = (cot_col * (grown - hot)).astype(BF16)

    packed = []
    for k in range(kinds):
        which = mine[:, kinds + k : kinds + k + 1]
        value = jnp.zeros((slots, BLOCK), BF16)
        for b in range(BLK_DEV):
            value = jnp.where(which == b + 1.0, grad[:, b * BLOCK : (b + 1) * BLOCK], value)
        packed.append(value)
    packed = jnp.concatenate(packed, axis=1)
    packed = lax.all_gather(packed, "dp", axis=0, tiled=True)

    back = lax.dot_general(
        grad, output_weight, (((1,), (1,)), ((), ())), preferred_element_type=F32
    ).astype(BF16)
    back = jnp.einsum(
        "sct,sch->sth", my_pick, back.reshape(n_vocab, capacity, width), preferred_element_type=F32
    ).astype(BF16)
    hidden_grad = lax.psum_scatter(
        back.reshape(n_vocab * tokens, width), "vocab", scatter_dimension=0, tiled=True
    )

    part_slots = jnp.einsum(
        "sct,sth->sch",
        pick,
        part_rows.reshape(blocks, tokens, part),
        preferred_element_type=F32,
    ).astype(BF16).reshape(n_dp * slots, part)
    spread = []
    for b in range(BLK_DEV):
        value = jnp.zeros((n_dp * slots, BLOCK), BF16)
        for k in range(kinds):
            value = jnp.where(
                all_only[:, k : k + 1] == b + 1.0, packed[:, k * BLOCK : (k + 1) * BLOCK], value
            )
        spread.append(value)
    spread = jnp.concatenate(spread, axis=1)
    weight_grad = lax.dot_general(
        part_slots, spread, (((0,), (0,)), ((), ())), preferred_element_type=F32
    ).astype(BF16)
    return (hidden_grad, weight_grad)


def solution(mesh):
    placed = (
        P(("dp", "vocab"), None),
        P(None, "vocab"),
        P(("dp", "vocab"), None),
        P(("dp", "vocab"), None, None),
        P(("dp", "vocab"), None, None),
        P(("dp", "vocab")),
        P(("dp", "vocab")),
        P(("dp", "vocab")),
        P(("dp", "vocab")),
    )
    return jax.shard_map(
        body,
        mesh=mesh,
        in_specs=placed,
        out_specs=(P(("dp", "vocab"), None), P("dp", "vocab")),
        check_vma=False,
    )
```

time: 278 us -> 245 us (0.88); the launches traced: 274 us -> 244 us
  blocking collectives: 0 us -> 72.6 us
  waiting for transfers between devices: 150 us -> 93 us
  local copies, waits for them, and re-layouts: 53.9 us -> 2.18 us
  starting transfers between devices: 14.9 us -> 0.34 us
  matrix products: 28.7 us -> 40 us
  other arithmetic: 11 us -> 22 us
    all_to_all x3 -> x0, waiting for transfers between devices: 97.8 us -> none  [the longest x1 49.1 us: body(): lax.all_to_all(grad_rows, 'vocab', split_axis=0, concat_axis=0, tiled=True)]
    all_gather x0 -> x3, waiting for transfers between devices: none -> 41.4 us  [the longest x1 32.6 us: body(): packed = lax.all_gather(packed, 'dp', axis=0, tiled=True)]
    all_gather x0 -> x1, blocking collectives: none -> 40.7 us  [body(): facts = lax.all_gather(facts, ('dp', 'vocab'), axis=0, tiled=False)]
    all_to_all x0 -> x1, blocking collectives: none -> 32 us  [body(): lax.all_to_all(hidden, 'dp', split_axis=1, concat_axis=0, tiled=True)]
    gather x6 -> x0, local copies, waits for them, and re-layouts: 29.9 us -> none  [the longest x2 18.3 us: body(): returned.reshape(slot_total, model_width)[slot_index].astype(jnp.float32)]
    scatter x2 -> x0, local copies, waits for them, and re-layouts: 18.1 us -> none  [the longest x1 16.6 us: body(): send_rows = jnp.zeros((slot_total, model_width), jnp.bfloat16).at[slot_in...]
    unnamed x0 -> x7, other arithmetic: none -> 15.7 us
    all_to_all x3 -> x0, starting transfers between devices: 14.9 us -> none  [the longest x1 5.4 us: body(): lax.all_to_all(send_meta, 'vocab', split_axis=0, concat_axis=0, tiled=True)]
  transfers between devices with their start and end apart: 4 -> 4, of which waited for: 3 -> 3; matrix products, arithmetic and copies ran while one was open for 20% -> 26% of each run, Pallas kernels for 0% -> 0%
where the time goes in v1:
time: 245 us; the launch traced here: 244 us
  waiting for transfers between devices  93 us (38%)
  blocking collectives  72.6 us (30%)
  matrix products  40 us (16%)
  other arithmetic  22 us (9%)
  between operations  14.2 us (6%)
    reduce_scatter x1, waiting for transfers between devices, body(): lax.psum_scatter(back.reshape(n_vocab * tokens, width), 'vocab', scatter_...  50.9 us
    all_gather x1, blocking collectives, body(): facts = lax.all_gather(facts, ('dp', 'vocab'), axis=0, tiled=False)  40.7 us
    all_gather x1, waiting for transfers between devices, body(): packed = lax.all_gather(packed, 'dp', axis=0, tiled=True)  32.6 us
    all_to_all x1, blocking collectives, body(): lax.all_to_all(hidden, 'dp', split_axis=1, concat_axis=0, tiled=True)  32 us
    unnamed x7, other arithmetic  15.7 us
    all_gather x1, waiting for transfers between devices, body(): lax.all_gather(part_rows.reshape(n_dp, tokens, part), 'vocab', axis=1)  8.72 us
    dot_general x1, matrix products, body(): scores = jnp.dot(rows, output_weight, preferred_element_type=F32)  8.7 us
    dot_general x1, matrix products, body(): lax.dot_general(grad, output_weight, (((1,), (1,)), ((), ())), preferred_...  8.19 us
  transfers between devices with their start and end apart: 4, of which 3 were waited for; matrix products, arithmetic and copies ran while one was open for 26% of the time, Pallas kernels for 0%

profile of v1, /device:TPU:0, one launch (start us, length us, event | category | flops | bytes accessed | tf_op | source)
XLA Modules:
  0.0 244.4 jit_solution(17321458530008942813)
XLA Ops:
  8.0 1.3 copy.20
  9.3 32.0 %all_to_all.16 = bf16[128,4,1024]{2,0,1:T(8,128)(2,1)} all-to-all(bf16[128,4,1024]{2,0,1:T(8,128)(2,1)S(1)} %bitcast.55), channel_id=1, replica_groups=mesh['dp'=4,'vocab'=8] {'dp'}, dimensions={1} | all-to-all | bytes 2097152 | tf_op jit(solution)/shard_map/all_to_all | solution.py:50
  41.7 40.7 %all-gather.3 = bf16[32,19,128]{2,1,0:T(8,128)(2,1)S(1)} all-gather(bf16[1,19,128]{2,1,0:T(8,128)(2,1)S(1)} %bitcast.56), channel_id=2, replica_groups=mesh['dp'=4,'vocab'=8] {'dp','vocab'}, dimensions={0}, use_global_device_ids=true | all-gather | bytes 160512 | tf_op jit(solution)/shard_map/all_gather | solution.py:46
  84.4 4.6 %convolution_convert_fusion.2 = bf16[8,64,4096]{2,1,0:T(8,128)(2,1)S(1)} fusion(bf16[8,128,4096]{2,1,0:T(8,128)(2,1)} %bitcast.48, pred[32,64,128]{2,1,0:T(32,128)(4,1)S(1)} %broadcast_compare_fusion, s32[]{:T(128)S(6)} %select_n.256), kind=kOutput, calls=%fused_computation.2 | convolution fusion | flops 538968064 | bytes 12648452 | tf_op jit(solution)/shard_map/sct,sth->sch/dot_general | solution.py:86
  89.1 8.7 %multiply_convert_fusion = bf16[512,1024]{1,0:T(8,128)(2,1)S(1)} fusion(bf16[512,4096]{1,0:T(8,128)(2,1)S(1)} %bitcast.49, bf16[4096,1024]{1,0:T(8,128)(2,1)} %param.10, f32[1024]{0:T(1024)S(1)} %get-tuple-element.78, f32[512]{0:T(512)S(1)} %bitcast.61, f32[1024]{0:T(1024)S(1)} %get-tuple-element.77, f32[512]{0:T(512)S(1)} %bitcast.64, f32[512]{0:T(512)S(1)} %bitcast.60, ...), kind=kOutput, calls=%fused_computation.8 | convolution fusion | flops 4304404480 | bytes 13651968 | tf_op jit(solution)/shard_map/dot_general | solution.py:88
  97.8 0.8 select_select_fusion
  98.5 0.8 select_select_fusion.1
  99.3 0.8 select_select_fusion.2
  100.1 0.8 pad_maximum_fusion
  101.1 8.2 %convolution_convert_fusion.1 = bf16[512,4096]{1,0:T(8,128)(2,1)S(1)} fusion(bf16[512,1024]{1,0:T(8,128)(2,1)S(1)} %multiply_convert_fusion, bf16[4096,1024]{1,0:T(8,128)(2,1)} %param.10), kind=kOutput, calls=%fused_computation.1 | convolution fusion | flops 4297064448 | bytes 13631488 | tf_op jit(solution)/shard_map/dot_general | solution.py:113
  109.3 5.6 %convolution_convert_fusion = bf16[8,128,4096]{2,1,0:T(8,128)(2,1)} fusion(bf16[8,64,4096]{2,1,0:T(8,128)(2,1)S(1)} %bitcast.52, pred[32,64,128]{2,1,0:T(32,128)(4,1)S(1)} %broadcast_compare_fusion, s32[]{:T(128)S(6)} %select_n.256), kind=kOutput, calls=%fused_computation | convolution fusion | flops 541065216 | bytes 12648452 | tf_op jit(solution)/shard_map/sct,sch->sth/dot_general | solution.py:116
  115.7 8.7 %all-gather.12.cloned.1.call-done = bf16[4,1024,1024]{2,1,0:T(8,128)(2,1)} async-done(((bf16[4,128,1024]{2,1,0:T(8,128)(2,1)}), bf16[4,1024,1024]{2,1,0:T(8,128)(2,1)}) %all-gather.12.cloned.1.call-update) | async-done | bytes 8388624 | tf_op jit(solution)/shard_map/all_gather | solution.py:51
  124.4 6.6 %convolution_convert_fusion.3 = bf16[32,64,1024]{2,1,0:T(8,128)(2,1)} fusion(bf16[32,128,1024]{2,1,0:T(8,128)(2,1)} %bitcast.50, f32[32,128]{1,0:T(8,128)S(1)} %convolution_select_fusion, f32[64]{0:T(128)S(1)} %iota_convert_fusion), kind=kOutput, calls=%fused_computation.3 | convolution fusion | flops 539230208 | bytes 12599552 | tf_op jit(solution)/shard_map/sct,sth->sch/dot_general | solution.py:123
  131.0 32.6 %all-gather.8.cloned.1.call-done = bf16[2048,384]{1,0:T(8,128)(2,1)} async-done(((bf16[512,384]{1,0:T(8,128)(2,1)}), bf16[2048,384]{1,0:T(8,128)(2,1)}) %all-gather.8.cloned.1.call-update) | async-done | bytes 1572880 | tf_op jit(solution)/shard_map/all_gather | solution.py:111
  163.6 3.5 %select_dynamic-update-slice_fusion.7 = bf16[2048,1024]{1,0:T(8,128)(2,1)S(1)} fusion(pred[2048]{0:T(1024)(128)(4,1)S(1)} %get-tuple-element.58, pred[2048]{0:T(1024)(128)(4,1)S(1)} %get-tuple-element.57, pred[2048]{0:T(1024)(128)(4,1)S(1)} %get-tuple-element.56, bf16[2048,384]{1,0:T(8,128)(2,1)} %all-gather.8.cloned.1.call-done), kind=kLoop, calls=%fused_computation.22 | loop fusion | flops 786431 | bytes 2103296
  167.1 3.4 %select_dynamic-update-slice_fusion.6 = bf16[2048,1024]{1,0:T(8,128)(2,1)S(1)} fusion(bf16[2048,1024]{1,0:T(8,128)(2,1)S(1)} %select_dynamic-update-slice_fusion.7, pred[2048]{0:T(1024)(128)(4,1)S(1)} %get-tuple-element.16, pred[2048]{0:T(1024)(128)(4,1)S(1)} %get-tuple-element.9, pred[2048]{0:T(1024)(128)(4,1)S(1)} %get-tuple-element.3, ...), kind=kLoop, calls=%fused_computation.21 | loop fusion | flops 786432 | bytes 2103296
  170.5 1.8 select_dynamic-update-slice_fusion.5
  172.3 1.8 select_dynamic-update-slice_fusion.4
  174.1 1.8 select_dynamic-update-slice_fusion.3
  175.9 1.8 select_dynamic-update-slice_fusion.2
  177.6 1.8 select_dynamic-update-slice_fusion.1
  179.4 1.8 select_dynamic-update-slice_fusion
  181.2 5.7 %convolution_convert_fusion.4 = bf16[1024,1024]{1,0:T(8,128)(2,1)} fusion(bf16[2048,1024]{1,0:T(8,128)(2,1)S(1)} %bitcast.51, bf16[2048,1024]{1,0:T(8,128)(2,1)S(1)} %select_dynamic-update-slice_fusion), kind=kOutput, calls=%fused_computation.9 | convolution fusion | flops 4296015872 | bytes 10485760 | tf_op jit(solution)/shard_map/dot_general | solution.py:138
  187.0 50.9 %reduce-scatter.2.cloned.1.call-done = bf16[128,4096]{1,0:T(8,128)(2,1)} async-done(((bf16[1024,4096]{1,0:T(8,128)(2,1)}), bf16[128,4096]{1,0:T(8,128)(2,1)}) %reduce-scatter.2.cloned.1.call-update) | async-done | bytes 1048592 | tf_op jit(solution)/shard_map/reduce_scatter | solution.py:119
  (54 shorter events, 4.0 us)
Async XLA Ops:
  7.2 34.2 %copy-start.2 = (s32[128,3,2]{0,2,1:T(2,128)S(1)}, s32[128,3,2]{0,2,1:T(2,128)}, u32[]{:S(2)}) copy-start(s32[128,3,2]{0,2,1:T(2,128)} %param.12) | copy-start | bytes 9220
  7.2 34.3 %copy-start.3 = (s32[128,3,2]{0,2,1:T(2,128)S(1)}, s32[128,3,2]{0,2,1:T(2,128)}, u32[]{:S(2)}) copy-start(s32[128,3,2]{0,2,1:T(2,128)} %param.13) | copy-start | bytes 9220
  7.2 34.3 %copy-start.5 = (s32[128]{0:T(128)S(1)}, s32[128]{0:T(128)}, u32[]{:S(2)}) copy-start(s32[128]{0:T(128)} %param.15) | copy-start | bytes 1540
  7.2 34.3 %copy-start.6 = (s32[128]{0:T(128)S(1)}, s32[128]{0:T(128)}, u32[]{:S(2)}) copy-start(s32[128]{0:T(128)} %param.14) | copy-start | bytes 1540
  7.2 34.3 %copy-start.4 = (s32[128,3]{0,1:T(4,128)S(1)}, s32[128,3]{0,1:T(4,128)}, u32[]{:S(2)}) copy-start(s32[128,3]{0,1:T(4,128)} %param.11) | copy-start | bytes 4612
  7.2 34.3 %copy-start.7 = (bf16[128]{0:T(256)(128)(2,1)S(1)}, bf16[128]{0:T(256)(128)(2,1)}, u32[]{:S(2)}) copy-start(bf16[128]{0:T(256)(128)(2,1)} %param.16) | copy-start | bytes 772
  7.2 34.3 %copy-start.8 = (bf16[128]{0:T(256)(128)(2,1)S(1)}, bf16[128]{0:T(256)(128)(2,1)}, u32[]{:S(2)}) copy-start(bf16[128]{0:T(256)(128)(2,1)} %param.17) | copy-start | bytes 772
  7.2 77.2 %all-gather.10.cloned.1.call-start = ((), (), s32[]{:S(2)}) async-start(), calls=%async_computation.4 | async-start | bytes 9437184 | tf_op jit(solution)/shard_map/all_gather | solution.py:49
  8.0 116.4 %all-gather.12.cloned.1.call-start = ((), (), s32[]{:S(2)}) async-start(), calls=%async_computation.5 | async-start | bytes 9437184 | tf_op jit(solution)/shard_map/all_gather | solution.py:51
  41.3 122.3 %all-gather.8.cloned.1.call-start = ((), (), s32[]{:S(2)}) async-start(), calls=%async_computation.3 | async-start | bytes 1966080 | tf_op jit(solution)/shard_map/all_gather | solution.py:111
  100.9 137.0 %reduce-scatter.2.cloned.1.call-start = ((), (), s32[]{:S(2)}) async-start(), calls=%async_computation.2 | async-start | bytes 9437184 | tf_op jit(solution)/shard_map/reduce_scatter | solution.py:119
  163.6 6.9 %copy-start = (bf16[2048,384]{1,0:T(8,128)(2,1)S(1)}, bf16[2048,384]{1,0:T(8,128)(2,1)}, u32[]{:S(2)}) copy-start(bf16[2048,384]{1,0:T(8,128)(2,1)} %all-gather.8.cloned.1.call-done) | copy-start | bytes 4718596
  174.1 7.1 %copy-start.1 = (bf16[32,64,1024]{2,1,0:T(8,128)(2,1)S(1)}, bf16[32,64,1024]{2,1,0:T(8,128)(2,1)}, u32[]{:S(2)}) copy-start(bf16[32,64,1024]{2,1,0:T(8,128)(2,1)} %convolution_convert_fusion.3) | copy-start | bytes 12582916
Sparse Core Ops, SparseCore 0:
  9.9 58.0 all-gather.9
  70.0 54.3 all-gather.11
  126.5 37.0 all-gather.7
  167.5 70.3 reduce-scatter.1

commit v2 on v1

--- a/solution.py
+++ b/solution.py
@@ -1,12 +1,252 @@
 import jax
 import jax.numpy as jnp
 from jax import lax
+from jax.experimental import pallas as pl
+from jax.experimental.pallas import tpu as pltpu
 from jax.sharding import PartitionSpec as P
 
 BLOCK = 128
 BLK_DEV = 8
 F32 = jnp.float32
 BF16 = jnp.bfloat16
+
+
+MESH = pl.DeviceIdType.MESH
+CUBE = 8
+
+
+def cube_peers():
+    v = lax.axis_index("vocab")
+    core = v % 2
+    x = (v // 2) % 2
+    y = v // 4
+    return v, v + 1 - 2 * core, v + 2 - 4 * x, v + 4 - 8 * y
+
+
+def greet(vocab_peers, dp_peers):
+    barrier = pltpu.get_barrier_semaphore()
+    for peer in vocab_peers:
+        pl.semaphore_signal(barrier, inc=1, device_id={"vocab": peer}, device_id_type=MESH)
+    for peer in dp_peers:
+        pl.semaphore_signal(barrier, inc=1, device_id={"dp": peer}, device_id_type=MESH)
+    pl.semaphore_wait(barrier, len(vocab_peers) + len(dp_peers))
+
+
+def front_kernel(n_dp, h_ref, f_ref, g_ref, p_ref, fo_ref, send, recv, local):
+    v, sib, xp, yp = cube_peers()
+    diag = xp + yp - v
+    dp = lax.axis_index("dp")
+    tokens, width = h_ref.shape
+    part = width // n_dp
+    half = tokens // 2
+    others = [(v + u) % CUBE for u in range(1, CUBE)]
+    groups = [(dp + n_dp - k) % n_dp for k in range(1, n_dp)]
+    greet(others, groups)
+    used = [0]
+
+    def push(src, dst, **where):
+        i = used[0]
+        used[0] += 1
+        copy = pltpu.make_async_remote_copy(
+            src_ref=src,
+            dst_ref=dst,
+            send_sem=send.at[i],
+            recv_sem=recv.at[i],
+            device_id=where,
+            device_id_type=MESH,
+        )
+        copy.start()
+        copies.append(copy)
+        return copy
+
+    copies = []
+    low, high = pl.ds(0, half), pl.ds(half, half)
+    keep_rows = pltpu.make_async_copy(h_ref, g_ref.at[v], local.at[0])
+    keep_rows.start()
+    keep_facts = pltpu.make_async_copy(f_ref, fo_ref.at[v, 0], local.at[1])
+    keep_facts.start()
+    facts_in = [push(f_ref, fo_ref.at[v, k + 1], dp=groups[k]) for k in range(n_dp - 1)]
+    x_low = push(h_ref.at[low], g_ref.at[v, low], vocab=xp)
+    y_high = push(h_ref.at[high], g_ref.at[v, high], vocab=yp)
+    x_high = push(h_ref.at[high], g_ref.at[v, high], vocab=xp)
+    y_low = push(h_ref.at[low], g_ref.at[v, low], vocab=yp)
+    s_own = push(h_ref, g_ref.at[v], vocab=sib)
+    parts_in = []
+    for k in range(n_dp - 1):
+        columns = pl.ds(pl.multiple_of(groups[k] * part, part), part)
+        parts_in.append(push(h_ref.at[:, columns], p_ref.at[k], dp=groups[k]))
+    for copy in facts_in:
+        copy.wait_recv()
+    keep_facts.wait()
+    facts_out = [push(fo_ref.at[v], fo_ref.at[v], vocab=peer) for peer in others]
+    x_low.wait_recv()
+    d_low = push(g_ref.at[xp, low], g_ref.at[xp, low], vocab=yp)
+    s1 = push(g_ref.at[xp, low], g_ref.at[xp, low], vocab=sib)
+    y_high.wait_recv()
+    d_high = push(g_ref.at[yp, high], g_ref.at[yp, high], vocab=xp)
+    s2 = push(g_ref.at[yp, high], g_ref.at[yp, high], vocab=sib)
+    x_high.wait_recv()
+    s3 = push(g_ref.at[xp, high], g_ref.at[xp, high], vocab=sib)
+    y_low.wait_recv()
+    s4 = push(g_ref.at[yp, low], g_ref.at[yp, low], vocab=sib)
+    d_low.wait_recv()
+    s5 = push(g_ref.at[diag, low], g_ref.at[diag, low], vocab=sib)
+    d_high.wait_recv()
+    s6 = push(g_ref.at[diag, high], g_ref.at[diag, high], vocab=sib)
+    for copy in [s_own, s1, s2, s3, s4, s5, s6] + parts_in + facts_out:
+        copy.wait_recv()
+    for copy in copies:
+        copy.wait_send()
+    keep_rows.wait()
+
+
+def front(hidden, facts, n_dp):
+    tokens, width = hidden.shape
+    total = 2 * (n_dp - 1) + 5 + (CUBE - 1) + 8
+    return pl.pallas_call(
+        lambda *refs: front_kernel(n_dp, *refs),
+        out_shape=(
+            jax.ShapeDtypeStruct((CUBE, tokens, width), BF16),
+            jax.ShapeDtypeStruct((n_dp - 1, tokens, width // n_dp), BF16),
+            jax.ShapeDtypeStruct((CUBE, n_dp) + facts.shape, BF16),
+        ),
+        in_specs=[pl.BlockSpec(memory_space=pltpu.VMEM)] * 2,
+        out_specs=(pl.BlockSpec(memory_space=pl.ANY),) * 3,
+        scratch_shapes=[
+            pltpu.SemaphoreType.DMA((total,)),
+            pltpu.SemaphoreType.DMA((total,)),
+            pltpu.SemaphoreType.DMA((2,)),
+        ],
+        compiler_params=pltpu.CompilerParams(collective_id=0, has_side_effects=True),
+        name="front",
+    )(hidden, facts)
+
+
+def add_rows(out_ref, first, rows, *parts):
+    step = 16
+
+    @pl.loop(0, rows // step)
+    def _(i):
+        at = pl.ds(pl.multiple_of(first + i * step, step), step)
+        total = parts[0](i * step, step).astype(F32)
+        for item in parts[1:]:
+            total = total + item(i * step, step).astype(F32)
+        out_ref[at, :] = total.astype(BF16)
+
+
+def rows_of(ref, first):
+    return lambda start, count: ref[pl.ds(pl.multiple_of(first + start, count), count), :]
+
+
+def back_kernel(n_dp, b_ref, k_ref, o_ref, ko_ref, sbuf, sums, hx, hy, fx, fy, send, recv, local):
+    v, sib, xp, yp = cube_peers()
+    diag = xp + yp - v
+    shift = sib - v
+    dp = lax.axis_index("dp")
+    tokens = o_ref.shape[0]
+    half = tokens // 2
+    groups = [(dp + n_dp - k) % n_dp for k in range(1, n_dp)]
+    greet([sib, xp, yp], groups)
+    copies = []
+
+    def push(src, dst, **where):
+        i = len(copies)
+        copy = pltpu.make_async_remote_copy(
+            src_ref=src,
+            dst_ref=dst,
+            send_sem=send.at[i],
+            recv_sem=recv.at[i],
+            device_id=where,
+            device_id_type=MESH,
+        )
+        copy.start()
+        copies.append(copy)
+        return copy
+
+    keep = pltpu.make_async_copy(k_ref, ko_ref.at[0], local.at[0])
+    keep.start()
+    order = [diag, xp, yp, v]
+    pair = [push(b_ref.at[q + shift], sbuf.at[i], vocab=sib) for i, q in enumerate(order)]
+    packs = [push(k_ref, ko_ref.at[k + 1], dp=groups[k]) for k in range(n_dp - 1)]
+    low, high = pl.ds(0, half), pl.ds(half, half)
+
+    def add_pair(i, first):
+        add_rows(
+            sums.at[i], first, half, rows_of(b_ref.at[order[i]], first), rows_of(sbuf.at[i], first)
+        )
+
+    def add_hop(i, first, hop):
+        add_rows(
+            sums.at[i],
+            first,
+            half,
+            rows_of(b_ref.at[order[i]], first),
+            rows_of(sbuf.at[i], first),
+            rows_of(hop, 0),
+        )
+
+    pair[0].wait_recv()
+    add_pair(0, 0)
+    to_x = push(sums.at[0, low], hx, vocab=xp)
+    add_pair(0, half)
+    to_y = push(sums.at[0, high], hy, vocab=yp)
+    pair[1].wait_recv()
+    add_pair(1, 0)
+    x_low = push(sums.at[1, low], fx.at[low], vocab=xp)
+    pair[2].wait_recv()
+    add_pair(2, half)
+    y_high = push(sums.at[2, high], fy.at[high], vocab=yp)
+    to_y.wait_recv()
+    add_hop(1, half, hy)
+    x_high = push(sums.at[1, high], fx.at[high], vocab=xp)
+    to_x.wait_recv()
+    add_hop(2, 0, hx)
+    y_low = push(sums.at[2, low], fy.at[low], vocab=yp)
+    pair[3].wait_recv()
+    for copy in (x_low, x_high, y_low, y_high):
+        copy.wait_recv()
+    add_rows(
+        o_ref,
+        0,
+        tokens,
+        rows_of(b_ref.at[v], 0),
+        rows_of(sbuf.at[3], 0),
+        rows_of(fx, 0),
+        rows_of(fy, 0),
+    )
+    for copy in packs:
+        copy.wait_recv()
+    for copy in copies:
+        copy.wait_send()
+    keep.wait()
+
+
+def back_sum(back, packed, n_dp):
+    tokens, width = back.shape[1:]
+    total = 4 + 6 + n_dp - 1
+    vmem = pl.BlockSpec(memory_space=pltpu.VMEM)
+    return pl.pallas_call(
+        lambda *refs: back_kernel(n_dp, *refs),
+        out_shape=(
+            jax.ShapeDtypeStruct((tokens, width), BF16),
+            jax.ShapeDtypeStruct((n_dp,) + packed.shape, BF16),
+        ),
+        in_specs=[vmem, vmem],
+        out_specs=(vmem, pl.BlockSpec(memory_space=pl.ANY)),
+        scratch_shapes=[
+            pltpu.VMEM((4, tokens, width), BF16),
+            pltpu.VMEM((3, tokens, width), BF16),
+            pltpu.VMEM((tokens // 2, width), BF16),
+            pltpu.VMEM((tokens // 2, width), BF16),
+            pltpu.VMEM((tokens, width), BF16),
+            pltpu.VMEM((tokens, width), BF16),
+            pltpu.SemaphoreType.DMA((total,)),
+            pltpu.SemaphoreType.DMA((total,)),
+            pltpu.SemaphoreType.DMA((1,)),
+        ],
+        compiler_params=pltpu.CompilerParams(collective_id=1, has_side_effects=True),
+        name="back_sum",
+    )(back, packed)
 
 
 def body(
@@ -43,12 +283,20 @@
         axis=0,
     ).astype(BF16)
     facts = jnp.concatenate([facts, log_norm[None, :], cotangent[None, :]], axis=0)
-    facts = lax.all_gather(facts, ("dp", "vocab"), axis=0, tiled=False)
+    facts = jnp.pad(facts, ((0, -facts.shape[0] % 16), (0, 0)))
     blocks = n_dp * n_vocab
 
-    group_rows = lax.all_gather(hidden, "vocab", axis=0, tiled=False)
-    part_rows = lax.all_to_all(hidden, "dp", split_axis=1, concat_axis=0, tiled=True)
-    part_rows = lax.all_gather(part_rows.reshape(n_dp, tokens, part), "vocab", axis=1)
+    cube = n_vocab == CUBE
+    if cube:
+        group_rows, part_rows, facts = front(hidden, facts, n_dp)
+    else:
+        group_rows = lax.all_gather(hidden, "vocab", axis=0, tiled=False)
+        part_rows = lax.all_to_all(hidden, "dp", split_axis=1, concat_axis=0, tiled=True)
+        part_rows = jnp.roll(part_rows.reshape(n_dp, tokens, part), -my_dp, axis=0)[1:]
+        facts = lax.all_gather(lax.all_gather(facts, "dp", axis=0), "vocab", axis=0)
+        facts = jnp.roll(facts, -my_dp, axis=1)
+    part_rows = lax.all_gather(part_rows, "vocab", axis=1)
+    facts = jnp.swapaxes(facts, 0, 1).reshape(blocks, -1, tokens)
 
     f = facts.astype(F32)
     pairs = visits * per_own
@@ -80,8 +328,8 @@
     slot_facts = jnp.einsum("sct,sat->sca", pick, attrs, preferred_element_type=F32)
     kinds = per_own + 1
     all_only = slot_facts[:, :, kinds : 2 * kinds].reshape(n_dp * slots, kinds)
-    mine = lax.dynamic_slice_in_dim(slot_facts, my_dp * n_vocab, n_vocab, 0).reshape(slots, -1)
-    my_pick = lax.dynamic_slice_in_dim(pick, my_dp * n_vocab, n_vocab, 0)
+    mine = slot_facts[:n_vocab].reshape(slots, -1)
+    my_pick = pick[:n_vocab]
 
     rows = jnp.einsum("sct,sth->sch", my_pick, group_rows, preferred_element_type=F32)
     rows = rows.astype(BF16).reshape(slots, width)
@@ -108,24 +356,29 @@
             value = jnp.where(which == b + 1.0, grad[:, b * BLOCK : (b + 1) * BLOCK], value)
         packed.append(value)
     packed = jnp.concatenate(packed, axis=1)
-    packed = lax.all_gather(packed, "dp", axis=0, tiled=True)
-
     back = lax.dot_general(
         grad, output_weight, (((1,), (1,)), ((), ())), preferred_element_type=F32
     ).astype(BF16)
     back = jnp.einsum(
         "sct,sch->sth", my_pick, back.reshape(n_vocab, capacity, width), preferred_element_type=F32
     ).astype(BF16)
-    hidden_grad = lax.psum_scatter(
-        back.reshape(n_vocab * tokens, width), "vocab", scatter_dimension=0, tiled=True
-    )
+    if cube:
+        hidden_grad, packed = back_sum(back, packed, n_dp)
+    else:
+        hidden_grad = lax.psum_scatter(
+            back.reshape(n_vocab * tokens, width), "vocab", scatter_dimension=0, tiled=True
+        )
+        packed = jnp.roll(lax.all_gather(packed, "dp", axis=0), -my_dp, axis=0)
+    packed = packed.reshape(n_dp * slots, kinds * BLOCK)
 
     part_slots = jnp.einsum(
         "sct,sth->sch",
-        pick,
-        part_rows.reshape(blocks, tokens, part),
+        pick[n_vocab:],
+        part_rows.reshape(blocks - n_vocab, tokens, part),
         preferred_element_type=F32,
-    ).astype(BF16).reshape(n_dp * slots, part)
+    ).astype(BF16).reshape((n_dp - 1) * slots, part)
+    own_slots = lax.dynamic_slice_in_dim(rows, my_dp * part, part, 1)
+    part_slots = jnp.concatenate([own_slots, part_slots], axis=0)
     spread = []
     for b in range(BLK_DEV):
         value = jnp.zeros((n_dp * slots, BLOCK), BF16)

time: 245 us -> 182 us (0.74)
  Pallas kernels: 0 us -> 94.4 us
  waiting for transfers between devices: 93 us -> 0.02 us
  blocking collectives: 72.6 us -> 0 us
  other arithmetic: 22 us -> 29.4 us
  local copies, waits for them, and re-layouts: 2.18 us -> 5.37 us
    pallas_call x0 -> x2, Pallas kernels: none -> 94.4 us  [the longest x1 48 us: front(): pl.pallas_call(lambda *refs: front_kernel(n_dp, *refs), out_shape=(jax.Sh...]
    reduce_scatter x1 -> x0, waiting for transfers between devices: 50.9 us -> none  [body(): lax.psum_scatter(back.reshape(n_vocab * tokens, width), 'vocab', scatter_...]
    all_gather x3 -> x1, waiting for transfers between devices: 41.4 us -> 0.01 us  [body(): part_rows = lax.all_gather(part_rows, 'vocab', axis=1)]
    all_gather x1 -> x0, blocking collectives: 40.7 us -> none  [body(): facts = lax.all_gather(facts, ('dp', 'vocab'), axis=0, tiled=False)]
    all_to_all x1 -> x0, blocking collectives: 32 us -> none  [body(): lax.all_to_all(hidden, 'dp', split_axis=1, concat_axis=0, tiled=True)]
    unnamed x7 -> x8, other arithmetic: 15.7 us -> 19.8 us
    dot_general x1, matrix products: 8.19 us -> 4.97 us  [body(): lax.dot_general(grad, output_weight, (((1,), (1,)), ((), ())), preferred_...]
    dot_general x1, matrix products: 6.6 us -> 3.88 us  [body(): jnp.einsum('sct,sth->sch', pick[n_vocab:], part_rows.reshape(blocks - n_v...]
  transfers between devices with their start and end apart: 4 -> 1, of which waited for: 3 -> 0; matrix products, arithmetic and copies ran while one was open for 26% -> 31% of each run, Pallas kernels for 0% -> 26%
where the time goes in v2:
time: 182 us
  Pallas kernels  94.4 us (52%)
  matrix products  38.4 us (21%)
  other arithmetic  29.4 us (16%)
  between operations  14.3 us (8%)
  local copies, waits for them, and re-layouts  5.37 us (3%)
    pallas_call x1, Pallas kernels, front(): pl.pallas_call(lambda *refs: front_kernel(n_dp, *refs), out_shape=(jax.Sh...  48 us
    pallas_call x1, Pallas kernels, back_sum(): pl.pallas_call(lambda *refs: back_kernel(n_dp, *refs), out_shape=(jax.Sha...  46.4 us
    unnamed x8, other arithmetic  19.8 us
    dot_general x1, matrix products, body(): scores = jnp.dot(rows, output_weight, preferred_element_type=F32)  10.3 us
    dot_general x1, matrix products, body(): lax.dot_general(part_slots, spread, (((0,), (0,)), ((), ())), preferred_e...  8.01 us
    dot_general x1, matrix products, body(): jnp.einsum('sct,sch->sth', my_pick, back.reshape(n_vocab, capacity, width...  5.73 us
    dot_general x1, matrix products, body(): jnp.einsum('sct,sth->sch', my_pick, group_rows, preferred_element_type=F32)  5.01 us
    dot_general x1, matrix products, body(): lax.dot_general(grad, output_weight, (((1,), (1,)), ((), ())), preferred_...  4.97 us
  transfers between devices with their start and end apart: 1, of which 0 were waited for; matrix products, arithmetic and copies ran while one was open for 31% of the time, Pallas kernels for 26%

profile of v2, /device:TPU:0, one launch (start us, length us, event | category | flops | bytes accessed | tf_op | source)
XLA Modules:
  0.0 181.9 jit_solution(12899530981816566169)
XLA Ops:
  10.0 0.8 concatenate.15
  11.4 48.0 %front.1 = (bf16[8,128,4096]{2,1,0:T(8,128)(2,1)}, bf16[3,128,1024]{2,1,0:T(8,128)(2,1)}, bf16[8,4,32,128]{3,2,1,0:T(8,128)(2,1)}) custom-call(bf16[128,4096]{1,0:T(8,128)(2,1)} %refs_0_.1, bf16[32,128]{1,0:T(8,128)(2,1)} %pad.4.refs_1_), custom_call_target="tpu_custom_call" | custom-call | tf_op jit(solution)/shard_map/front/pallas_call | solution.py:106
  59.4 1.0 copy.11
  62.4 5.0 %convolution_convert_fusion.2 = bf16[8,64,4096]{2,1,0:T(8,128)(2,1)S(1)} fusion(bf16[8,128,4096]{2,1,0:T(8,128)(2,1)} %get-tuple-element.8, f32[32,128]{1,0:T(8,128)S(1)} %convolution_select_fusion, f32[64]{0:T(128)S(1)} %iota_convert_fusion), kind=kOutput, calls=%fused_computation.2 | convolution fusion | flops 539230208 | bytes 12599552 | tf_op jit(solution)/shard_map/sct,sth->sch/dot_general | solution.py:334
  67.4 10.3 %multiply_convert_fusion = bf16[512,1024]{1,0:T(8,128)(2,1)S(1)} fusion(bf16[512,4096]{1,0:T(8,128)(2,1)S(1)} %bitcast.51, bf16[4096,1024]{1,0:T(8,128)(2,1)} %param.10, f32[1024]{0:T(1024)S(1)} %get-tuple-element.88, f32[512]{0:T(512)S(1)} %bitcast.58, f32[1024]{0:T(1024)S(1)} %get-tuple-element.87, f32[512]{0:T(512)S(1)} %bitcast.61, ...), kind=kOutput, calls=%fused_computation.12 | convolution fusion | flops 4304404480 | bytes 13651968 | tf_op jit(solution)/shard_map/dot_general | solution.py:336
  77.7 0.8 select_select_fusion.2
  78.5 0.8 select_select_fusion.1
  79.2 0.8 select_select_fusion
  80.0 0.8 pad_maximum_fusion.refs_1_
  80.8 5.0 %convolution_convert_fusion.1 = bf16[512,4096]{1,0:T(8,128)(2,1)S(1)} fusion(bf16[512,1024]{1,0:T(8,128)(2,1)S(1)} %multiply_convert_fusion, bf16[4096,1024]{1,0:T(8,128)(2,1)S(1)} %bitcast.65), kind=kOutput, calls=%fused_computation.1 | convolution fusion | flops 4297064448 | bytes 13631488 | tf_op jit(solution)/shard_map/dot_general | solution.py:359
  85.8 5.7 %convolution_convert_fusion.refs_0_ = bf16[8,128,4096]{2,1,0:T(8,128)(2,1)} fusion(bf16[8,64,4096]{2,1,0:T(8,128)(2,1)S(1)} %bitcast.67, f32[32,128]{1,0:T(8,128)S(1)} %convolution_select_fusion, f32[64]{0:T(128)S(1)} %iota_convert_fusion), kind=kOutput, calls=%fused_computation | convolution fusion | flops 541327360 | bytes 12599552 | tf_op jit(solution)/shard_map/sct,sch->sth/dot_general | solution.py:362
  91.5 46.4 %back_sum.1 = (bf16[128,4096]{1,0:T(8,128)(2,1)}, bf16[4,512,384]{2,1,0:T(8,128)(2,1)}) custom-call(bf16[8,128,4096]{2,1,0:T(8,128)(2,1)} %convolution_convert_fusion.refs_0_, bf16[512,384]{1,0:T(8,128)(2,1)} %pad_maximum_fusion.refs_1_), custom_call_target="tpu_custom_call" | custom-call | tf_op jit(solution)/shard_map/back_sum/pallas_call | solution.py:228
  138.5 1.3 constant_dynamic-slice_fusion
  139.8 4.2 %select_dynamic-update-slice_fusion.7 = bf16[2048,1024]{1,0:T(8,128)(2,1)} fusion(pred[2048]{0:T(1024)(128)(4,1)S(1)} %get-tuple-element.68, pred[2048]{0:T(1024)(128)(4,1)S(1)} %get-tuple-element.67, pred[2048]{0:T(1024)(128)(4,1)S(1)} %get-tuple-element.66, bf16[2048,384]{1,0:T(8,128)(2,1)} %bitcast.42), kind=kLoop, calls=%fused_computation.27 | loop fusion | flops 786431 | bytes 2103296
  144.0 2.6 %select_dynamic-update-slice_fusion.6 = bf16[2048,1024]{1,0:T(8,128)(2,1)} fusion(bf16[2048,1024]{1,0:T(8,128)(2,1)} %select_dynamic-update-slice_fusion.7, pred[2048]{0:T(1024)(128)(4,1)S(1)} %get-tuple-element.26, pred[2048]{0:T(1024)(128)(4,1)S(1)} %get-tuple-element.19, pred[2048]{0:T(1024)(128)(4,1)S(1)} %get-tuple-element.13, ...), kind=kLoop, calls=%fused_computation.26 | loop fusion | flops 786432 | bytes 2103296
  146.6 2.6 %select_dynamic-update-slice_fusion.5 = bf16[2048,1024]{1,0:T(8,128)(2,1)} fusion(bf16[2048,1024]{1,0:T(8,128)(2,1)} %select_dynamic-update-slice_fusion.6, pred[2048]{0:T(1024)(128)(4,1)S(1)} %get-tuple-element.27, pred[2048]{0:T(1024)(128)(4,1)S(1)} %get-tuple-element.20, pred[2048]{0:T(1024)(128)(4,1)S(1)} %get-tuple-element.14, ...), kind=kLoop, calls=%fused_computation.25 | loop fusion | flops 786432 | bytes 2103296
  149.2 2.6 %select_dynamic-update-slice_fusion.4 = bf16[2048,1024]{1,0:T(8,128)(2,1)} fusion(bf16[2048,1024]{1,0:T(8,128)(2,1)} %select_dynamic-update-slice_fusion.5, pred[2048]{0:T(1024)(128)(4,1)S(1)} %get-tuple-element.28, pred[2048]{0:T(1024)(128)(4,1)S(1)} %get-tuple-element.21, pred[2048]{0:T(1024)(128)(4,1)S(1)} %get-tuple-element.15, ...), kind=kLoop, calls=%fused_computation.24 | loop fusion | flops 786432 | bytes 2103296
  151.8 2.6 %select_dynamic-update-slice_fusion.3 = bf16[2048,1024]{1,0:T(8,128)(2,1)} fusion(bf16[2048,1024]{1,0:T(8,128)(2,1)} %select_dynamic-update-slice_fusion.4, pred[2048]{0:T(1024)(128)(4,1)S(1)} %get-tuple-element.29, pred[2048]{0:T(1024)(128)(4,1)S(1)} %get-tuple-element.22, pred[2048]{0:T(1024)(128)(4,1)S(1)} %get-tuple-element.16, ...), kind=kLoop, calls=%fused_computation.23 | loop fusion | flops 786432 | bytes 2103296
  154.4 2.6 %select_dynamic-update-slice_fusion.2 = bf16[2048,1024]{1,0:T(8,128)(2,1)} fusion(bf16[2048,1024]{1,0:T(8,128)(2,1)} %select_dynamic-update-slice_fusion.3, pred[2048]{0:T(1024)(128)(4,1)S(1)} %get-tuple-element.30, pred[2048]{0:T(1024)(128)(4,1)S(1)} %get-tuple-element.23, pred[2048]{0:T(1024)(128)(4,1)S(1)} %get-tuple-element.17, ...), kind=kLoop, calls=%fused_computation.22 | loop fusion | flops 786432 | bytes 2103296
  157.0 2.6 %select_dynamic-update-slice_fusion.1 = bf16[2048,1024]{1,0:T(8,128)(2,1)} fusion(bf16[2048,1024]{1,0:T(8,128)(2,1)} %select_dynamic-update-slice_fusion.2, pred[2048]{0:T(1024)(128)(4,1)S(1)} %get-tuple-element.69, pred[2048]{0:T(1024)(128)(4,1)S(1)} %get-tuple-element.24, pred[2048]{0:T(1024)(128)(4,1)S(1)} %get-tuple-element.18, ...), kind=kLoop, calls=%fused_computation.21 | loop fusion | flops 786432 | bytes 2103296
  159.6 2.6 %select_dynamic-update-slice_fusion = bf16[2048,1024]{1,0:T(8,128)(2,1)} fusion(bf16[2048,1024]{1,0:T(8,128)(2,1)} %select_dynamic-update-slice_fusion.1, pred[2048]{0:T(1024)(128)(4,1)S(1)} %get-tuple-element.70, pred[2048]{0:T(1024)(128)(4,1)S(1)} %get-tuple-element.25, pred[2048]{0:T(1024)(128)(4,1)S(1)} %get-tuple-element.12, ...), kind=kLoop, calls=%fused_computation.20 | loop fusion | flops 786432 | bytes 2103296 | tf_op jit(solution)/shard_map/concatenate | solution.py:390
  162.2 3.9 %convolution_convert_fusion.3 = bf16[24,64,1024]{2,1,0:T(8,128)(2,1)S(1)} fusion(bf16[24,128,1024]{2,1,0:T(8,128)(2,1)} %bitcast.66, f32[32,128]{1,0:T(8,128)S(1)} %convolution_select_fusion, f32[64]{0:T(128)S(1)} %iota_convert_fusion), kind=kOutput, calls=%fused_computation.9 | convolution fusion | flops 404488192 | bytes 9453824 | tf_op jit(solution)/shard_map/sct,sth->sch/dot_general | solution.py:374
  166.1 8.0 %fusion.6 = bf16[1024,1024]{1,0:T(8,128)(2,1)} fusion(bf16[2048,1024]{1,0:T(8,128)(2,1)} %select_dynamic-update-slice_fusion, bf16[1536,1024]{1,0:T(8,128)(2,1)S(1)} %bitcast.68, bf16[512,1024]{1,0:T(8,128)(2,1)S(1)} %constant_dynamic-slice_fusion), kind=kOutput, calls=%fused_computation.13 | convolution fusion | flops 4304404480 | bytes 10485760 | tf_op jit(solution)/shard_map/dot_general | solution.py:391
  174.1 1.0 copy.22
  (40 shorter events, 5.9 us)
Async XLA Ops:
  7.2 155.0 %all-gather.3.cloned.1.call-start = ((), (), s32[]{:S(2)}) async-start(), calls=%async_computation | async-start | bytes 7077888 | tf_op jit(solution)/shard_map/all_gather | solution.py:298
  67.4 10.3 %copy-start.2 = (bf16[8,64,4096]{2,1,0:T(8,128)(2,1)}, bf16[8,64,4096]{2,1,0:T(8,128)(2,1)S(1)}, u32[]{:S(2)}) copy-start(bf16[8,64,4096]{2,1,0:T(8,128)(2,1)S(1)} %convolution_convert_fusion.2) | copy-start | bytes 12582916
  67.4 13.4 %slice-start = ((s8[8388608]{0:T(1024)(128)(4,1)}), s8[4194304]{0:T(1024)(128)(4,1)S(1)}, s32[]{:S(2)}) async-start(s8[8388608]{0:T(1024)(128)(4,1)} %bitcast.64), calls=%async_computation.1 | async-start | bytes 8388608
  67.4 13.4 %slice-start.1 = ((s8[8388608]{0:T(1024)(128)(4,1)}), s8[4194304]{0:T(1024)(128)(4,1)S(1)}, s32[]{:S(2)}) async-start(s8[8388608]{0:T(1024)(128)(4,1)} %bitcast.64), calls=%async_computation.2 | async-start | bytes 8388608
  137.9 6.1 %copy-start = (bf16[4,512,384]{2,1,0:T(8,128)(2,1)S(1)}, bf16[4,512,384]{2,1,0:T(8,128)(2,1)}, u32[]{:S(2)}) copy-start(bf16[4,512,384]{2,1,0:T(8,128)(2,1)} %get-tuple-element.11) | copy-start | bytes 4718596
  166.1 8.0 %copy-start.1 = (bf16[128,4096]{1,0:T(8,128)(2,1)S(1)}, bf16[128,4096]{1,0:T(8,128)(2,1)}, u32[]{:S(2)}) copy-start(bf16[128,4096]{1,0:T(8,128)(2,1)} %get-tuple-element.95) | copy-start | bytes 3145732
Sparse Core Ops, SparseCore 0:
  59.5 44.7 all-gather.2

commit v3 on v2

--- a/solution.py
+++ b/solution.py
@@ -249,6 +249,75 @@
     )(back, packed)
 
 
+def weight_kernel(own_ref, pick_ref, part_ref, packed_ref, only_ref, o_ref, lhs, lhs_t, acc):
+    g = pl.program_id(0)
+    sources, capacity = pick_ref.shape[:2]
+    kinds = only_ref.shape[1]
+    pair = 2 * BLOCK
+
+    @pl.when(g == 0)
+    def _():
+        lhs[...] = own_ref[...]
+        acc[...] = jnp.zeros_like(acc)
+
+    @pl.when(g > 0)
+    def _():
+        for s in range(sources):
+            lhs[s * capacity : (s + 1) * capacity, :] = jnp.dot(
+                pick_ref[s], part_ref[0, s], preferred_element_type=F32
+            ).astype(BF16)
+
+    lhs_t[...] = lhs[...].T
+
+    @pl.loop(0, acc.shape[1] // pair)
+    def _(j):
+        sides = []
+        for i in range(2):
+            block = (2 * j + i + 1).astype(F32)
+            value = jnp.zeros((lhs.shape[0], BLOCK), F32)
+            for k in range(kinds):
+                value = jnp.where(
+                    only_ref[:, k : k + 1] == block,
+                    packed_ref[0, :, k * BLOCK : (k + 1) * BLOCK].astype(F32),
+                    value,
+                )
+            sides.append(value.astype(BF16))
+        spread = jnp.concatenate(sides, axis=1)
+        at = pl.ds(pl.multiple_of(j * pair, pair), pair)
+        acc[:, at] += jnp.dot(lhs_t[...], spread, preferred_element_type=F32)
+
+    @pl.when(g == pl.num_programs(0) - 1)
+    def _():
+        o_ref[...] = acc[...].astype(BF16)
+
+
+def weight_product(own, pick, parts, packed, only, words):
+    groups, slots = packed.shape[:2]
+    _, sources, tokens, part = parts.shape
+    capacity = pick.shape[1]
+    kinds = only.shape[1]
+    return pl.pallas_call(
+        weight_kernel,
+        grid=(groups,),
+        out_shape=jax.ShapeDtypeStruct((part, words), BF16),
+        in_specs=[
+            pl.BlockSpec((slots, part), lambda g: (0, 0)),
+            pl.BlockSpec((sources, capacity, tokens), lambda g: (jnp.maximum(g - 1, 0), 0, 0)),
+            pl.BlockSpec((1, sources, tokens, part), lambda g: (jnp.maximum(g - 1, 0), 0, 0, 0)),
+            pl.BlockSpec((1, slots, packed.shape[2]), lambda g: (g, 0, 0)),
+            pl.BlockSpec((slots, kinds), lambda g: (g, 0)),
+        ],
+        out_specs=pl.BlockSpec((part, words), lambda g: (0, 0)),
+        scratch_shapes=[
+            pltpu.VMEM((slots, part), BF16),
+            pltpu.VMEM((part, slots), BF16),
+            pltpu.VMEM((part, words), F32),
+        ],
+        compiler_params=pltpu.CompilerParams(dimension_semantics=("arbitrary",)),
+        name="weight_product",
+    )(own, pick, parts, packed, only)
+
+
 def body(
     hidden,
     output_weight,
@@ -369,28 +438,8 @@
             back.reshape(n_vocab * tokens, width), "vocab", scatter_dimension=0, tiled=True
         )
         packed = jnp.roll(lax.all_gather(packed, "dp", axis=0), -my_dp, axis=0)
-    packed = packed.reshape(n_dp * slots, kinds * BLOCK)
-
-    part_slots = jnp.einsum(
-        "sct,sth->sch",
-        pick[n_vocab:],
-        part_rows.reshape(blocks - n_vocab, tokens, part),
-        preferred_element_type=F32,
-    ).astype(BF16).reshape((n_dp - 1) * slots, part)
     own_slots = lax.dynamic_slice_in_dim(rows, my_dp * part, part, 1)
-    part_slots = jnp.concatenate([own_slots, part_slots], axis=0)
-    spread = []
-    for b in range(BLK_DEV):
-        value = jnp.zeros((n_dp * slots, BLOCK), BF16)
-        for k in range(kinds):
-            value = jnp.where(
-                all_only[:, k : k + 1] == b + 1.0, packed[:, k * BLOCK : (k + 1) * BLOCK], value
-            )
-        spread.append(value)
-    spread = jnp.concatenate(spread, axis=1)
-    weight_grad = lax.dot_general(
-        part_slots, spread, (((0,), (0,)), ((), ())), preferred_element_type=F32
-    ).astype(BF16)
+    weight_grad = weight_product(own_slots, pick[n_vocab:], part_rows, packed, all_only, words)
     return (hidden_grad, weight_grad)
 
 

time: 182 us -> 174 us (0.956)
  Pallas kernels: 94.4 us -> 117 us
  other arithmetic: 29.4 us -> 7.59 us
  matrix products: 38.4 us -> 26.9 us
  local copies, waits for them, and re-layouts: 5.37 us -> 7.6 us
    pallas_call x0 -> x1, Pallas kernels: none -> 22.8 us  [weight_product(): pl.pallas_call(weight_kernel, grid=(groups,), out_shape=jax.ShapeDtypeStr...]
    unnamed x8 -> x1, other arithmetic: 19.8 us -> 0.01 us
    dot_general x2 -> x0, matrix products: 11.9 us -> none  [the longest x1 8.01 us: body(): lax.dot_general(part_slots, spread, (((0,), (0,)), ((), ())), preferred_e...]
    concatenate x1 -> x0, other arithmetic: 2.58 us -> none  [body(): spread = jnp.concatenate(spread, axis=1)]
  transfers between devices with their start and end apart: 1 -> 1, of which waited for: 0 -> 0; matrix products, arithmetic and copies ran while one was open for 31% -> 21% of each run, Pallas kernels for 26% -> 27%
where the time goes in v3:
time: 174 us; the launch traced here: 173 us
  Pallas kernels  117 us (67%)
  matrix products  26.9 us (15%)
  between operations  14.2 us (8%)
  local copies, waits for them, and re-layouts  7.6 us (4%)
  other arithmetic  7.59 us (4%)
    pallas_call x1, Pallas kernels, front(): pl.pallas_call(lambda *refs: front_kernel(n_dp, *refs), out_shape=(jax.Sh...  48 us
    pallas_call x1, Pallas kernels, back_sum(): pl.pallas_call(lambda *refs: back_kernel(n_dp, *refs), out_shape=(jax.Sha...  46.1 us
    pallas_call x1, Pallas kernels, weight_product(): pl.pallas_call(weight_kernel, grid=(groups,), out_shape=jax.ShapeDtypeStr...  22.8 us
    dot_general x1, matrix products, body(): scores = jnp.dot(rows, output_weight, preferred_element_type=F32)  10.3 us
    dot_general x1, matrix products, body(): jnp.einsum('sct,sch->sth', my_pick, back.reshape(n_vocab, capacity, width...  5.73 us
    dot_general x1, matrix products, body(): jnp.einsum('sct,sth->sch', my_pick, group_rows, preferred_element_type=F32)  5.34 us
    dot_general x1, matrix products, body(): lax.dot_general(grad, output_weight, (((1,), (1,)), ((), ())), preferred_...  4.96 us
  transfers between devices with their start and end apart: 1, of which 0 were waited for; matrix products, arithmetic and copies ran while one was open for 21% of the time, Pallas kernels for 27%

profile of v3, /device:TPU:0, one launch (start us, length us, event | category | flops | bytes accessed | tf_op | source)
XLA Modules:
  0.0 173.2 jit_solution(9945922148939189765)
XLA Ops:
  7.2 0.7 convert.44
  7.9 0.7 convert.45
  8.6 0.7 convert_bitcast_fusion
  9.3 0.7 convert_bitcast_fusion.1
  10.0 0.8 concatenate.9
  10.8 0.6 pad.4.refs_1_
  11.4 48.0 %front.1 = (bf16[8,128,4096]{2,1,0:T(8,128)(2,1)}, bf16[3,128,1024]{2,1,0:T(8,128)(2,1)}, bf16[8,4,32,128]{3,2,1,0:T(8,128)(2,1)}) custom-call(bf16[128,4096]{1,0:T(8,128)(2,1)} %refs_0_.1, bf16[32,128]{1,0:T(8,128)(2,1)} %pad.4.refs_1_), custom_call_target="tpu_custom_call" | custom-call | tf_op jit(solution)/shard_map/front/pallas_call | solution.py:106
  59.4 1.0 copy.12
  60.9 0.4 stack.4
  61.5 0.4 fusion.3
  62.1 1.4 copy.14
  63.6 5.3 %convolution_convert_fusion.2 = bf16[8,64,4096]{2,1,0:T(8,128)(2,1)S(1)} fusion(bf16[8,128,4096]{2,1,0:T(8,128)(2,1)} %get-tuple-element.8, f32[32,128]{1,0:T(8,128)S(1)} %convolution_select_fusion, f32[64]{0:T(128)S(1)} %iota_convert_fusion), kind=kOutput, calls=%fused_computation.2 | convolution fusion | flops 539230208 | bytes 12599552 | tf_op jit(solution)/shard_map/sct,sth->sch/dot_general | solution.py:403
  69.0 10.3 %multiply_convert_fusion = bf16[512,1024]{1,0:T(8,128)(2,1)S(1)} fusion(bf16[512,4096]{1,0:T(8,128)(2,1)S(1)} %bitcast.40, bf16[4096,1024]{1,0:T(8,128)(2,1)} %param.10, f32[1024]{0:T(1024)S(1)} %get-tuple-element.59, f32[512]{0:T(512)S(1)} %bitcast.47, f32[1024]{0:T(1024)S(1)} %get-tuple-element.58, f32[512]{0:T(512)S(1)} %bitcast.50, f32[512]{0:T(512)S(1)} %bitcast.46, ...), kind=kOutput, calls=%fused_computation.7 | convolution fusion | flops 4304404480 | bytes 13651968 | tf_op jit(solution)/shard_map/dot_general | solution.py:405
  79.3 0.8 select_select_fusion.2
  80.0 0.8 select_select_fusion.1
  80.8 0.8 select_select_fusion
  81.6 0.8 pad_maximum_fusion.refs_1_
  82.4 5.0 %convolution_convert_fusion.1 = bf16[512,4096]{1,0:T(8,128)(2,1)S(1)} fusion(bf16[512,1024]{1,0:T(8,128)(2,1)S(1)} %multiply_convert_fusion, bf16[4096,1024]{1,0:T(8,128)(2,1)S(1)} %bitcast.54), kind=kOutput, calls=%fused_computation.1 | convolution fusion | flops 4297064448 | bytes 13631488 | tf_op jit(solution)/shard_map/dot_general | solution.py:428
  87.4 5.7 %convolution_convert_fusion.refs_0_ = bf16[8,128,4096]{2,1,0:T(8,128)(2,1)} fusion(bf16[8,64,4096]{2,1,0:T(8,128)(2,1)S(1)} %bitcast.55, f32[32,128]{1,0:T(8,128)S(1)} %convolution_select_fusion, f32[64]{0:T(128)S(1)} %iota_convert_fusion), kind=kOutput, calls=%fused_computation | convolution fusion | flops 541327360 | bytes 12599552 | tf_op jit(solution)/shard_map/sct,sch->sth/dot_general | solution.py:431
  93.1 46.1 %back_sum.1 = (bf16[128,4096]{1,0:T(8,128)(2,1)}, bf16[4,512,384]{2,1,0:T(8,128)(2,1)}) custom-call(bf16[8,128,4096]{2,1,0:T(8,128)(2,1)} %convolution_convert_fusion.refs_0_, bf16[512,384]{1,0:T(8,128)(2,1)} %pad_maximum_fusion.refs_1_), custom_call_target="tpu_custom_call" | custom-call | tf_op jit(solution)/shard_map/back_sum/pallas_call | solution.py:228
  139.2 2.3 %constant_dynamic-slice_fusion.own_ref = bf16[512,1024]{1,0:T(8,128)(2,1)} fusion(bf16[512,4096]{1,0:T(8,128)(2,1)} %bitcast.41, s32[]{:T(128)S(6)} %select_n.223), kind=kLoop, calls=%fused_computation.91 | loop fusion | bytes 2097156 | tf_op jit(solution)/shard_map/dynamic_slice | solution.py:441
  141.7 0.9 slice_convert_fusion.pick_ref
  142.6 22.8 %weight_product.1 = bf16[1024,1024]{1,0:T(8,128)(2,1)} custom-call(bf16[512,1024]{1,0:T(8,128)(2,1)} %constant_dynamic-slice_fusion.own_ref, bf16[24,64,128]{2,1,0:T(8,128)(2,1)} %slice_convert_fusion.pick_ref, bf16[3,8,128,1024]{3,2,1,0:T(8,128)(2,1)} %bitcast.37, bf16[4,512,384]{2,1,0:T(8,128)(2,1)} %get-tuple-element.11.packed_ref, f32[2048,3]{1,0:T(8,128)} %bitcast.38), custom_call_target="tpu_custom_call" | custom-call | tf_op jit(solution)/shard_map/weight_product/pallas_call | solution.py:299
  165.4 1.0 copy.16
  (29 shorter events, 1.3 us)
Async XLA Ops:
  7.2 135.4 %all-gather.3.cloned.1.call-start = ((), (), s32[]{:S(2)}) async-start(), calls=%async_computation | async-start | bytes 7077888 | tf_op jit(solution)/shard_map/all_gather | solution.py:367
  69.0 10.3 %copy-start.1 = (bf16[8,64,4096]{2,1,0:T(8,128)(2,1)}, bf16[8,64,4096]{2,1,0:T(8,128)(2,1)S(1)}, u32[]{:S(2)}) copy-start(bf16[8,64,4096]{2,1,0:T(8,128)(2,1)S(1)} %convolution_convert_fusion.2) | copy-start | bytes 12582916
  69.0 13.4 %slice-start = ((s8[8388608]{0:T(1024)(128)(4,1)}), s8[4194304]{0:T(1024)(128)(4,1)S(1)}, s32[]{:S(2)}) async-start(s8[8388608]{0:T(1024)(128)(4,1)} %bitcast.53), calls=%async_computation.1 | async-start | bytes 8388608
  69.0 13.4 %slice-start.1 = ((s8[8388608]{0:T(1024)(128)(4,1)}), s8[4194304]{0:T(1024)(128)(4,1)S(1)}, s32[]{:S(2)}) async-start(s8[8388608]{0:T(1024)(128)(4,1)} %bitcast.53), calls=%async_computation.2 | async-start | bytes 8388608
  142.6 22.8 %copy-start = (bf16[128,4096]{1,0:T(8,128)(2,1)S(1)}, bf16[128,4096]{1,0:T(8,128)(2,1)}, u32[]{:S(2)}) copy-start(bf16[128,4096]{1,0:T(8,128)(2,1)} %get-tuple-element.66) | copy-start | bytes 3145732
Sparse Core Ops, SparseCore 0:
  59.5 44.5 all-gather.2

commit v4 on v3

--- a/solution.py
+++ b/solution.py
@@ -269,7 +269,7 @@
 
     lhs_t[...] = lhs[...].T
 
-    @pl.loop(0, acc.shape[1] // pair)
+    @pl.loop(0, acc.shape[1] // pair, unroll=True)
     def _(j):
         sides = []
         for i in range(2):

time: 174 us -> 167 us (0.960)
  Pallas kernels: 117 us -> 111 us
    pallas_call x1, Pallas kernels: 22.8 us -> 16.5 us  [weight_product(): pl.pallas_call(weight_kernel, grid=(groups,), out_shape=jax.ShapeDtypeStr...]
  transfers between devices with their start and end apart: 1 -> 1, of which waited for: 0 -> 0; matrix products, arithmetic and copies ran while one was open for 21% -> 22% of each run, Pallas kernels for 27% -> 28%
where the time goes in v4:
time: 167 us
  Pallas kernels  111 us (66%)
  matrix products  26.9 us (16%)
  between operations  14.2 us (9%)
  local copies, waits for them, and re-layouts  7.6 us (5%)
  other arithmetic  7.59 us (5%)
    pallas_call x1, Pallas kernels, front(): pl.pallas_call(lambda *refs: front_kernel(n_dp, *refs), out_shape=(jax.Sh...  48 us
    pallas_call x1, Pallas kernels, back_sum(): pl.pallas_call(lambda *refs: back_kernel(n_dp, *refs), out_shape=(jax.Sha...  46.1 us
    pallas_call x1, Pallas kernels, weight_product(): pl.pallas_call(weight_kernel, grid=(groups,), out_shape=jax.ShapeDtypeStr...  16.5 us
    dot_general x1, matrix products, body(): scores = jnp.dot(rows, output_weight, preferred_element_type=F32)  10.3 us
    dot_general x1, matrix products, body(): jnp.einsum('sct,sch->sth', my_pick, back.reshape(n_vocab, capacity, width...  5.73 us
    dot_general x1, matrix products, body(): jnp.einsum('sct,sth->sch', my_pick, group_rows, preferred_element_type=F32)  5.34 us
    dot_general x1, matrix products, body(): lax.dot_general(grad, output_weight, (((1,), (1,)), ((), ())), preferred_...  4.96 us
  transfers between devices with their start and end apart: 1, of which 0 were waited for; matrix products, arithmetic and copies ran while one was open for 22% of the time, Pallas kernels for 28%

profile of v4, /device:TPU:0, one launch (start us, length us, event | category | flops | bytes accessed | tf_op | source)
XLA Modules:
  0.0 166.9 jit_solution(11836336668041737508)
XLA Ops:
  7.2 0.7 convert.44
  7.9 0.7 convert.45
  8.6 0.7 convert_bitcast_fusion
  9.3 0.7 convert_bitcast_fusion.1
  10.0 0.8 concatenate.9
  10.8 0.6 pad.4.refs_1_
  11.4 48.0 %front.1 = (bf16[8,128,4096]{2,1,0:T(8,128)(2,1)}, bf16[3,128,1024]{2,1,0:T(8,128)(2,1)}, bf16[8,4,32,128]{3,2,1,0:T(8,128)(2,1)}) custom-call(bf16[128,4096]{1,0:T(8,128)(2,1)} %refs_0_.1, bf16[32,128]{1,0:T(8,128)(2,1)} %pad.4.refs_1_), custom_call_target="tpu_custom_call" | custom-call | tf_op jit(solution)/shard_map/front/pallas_call | solution.py:106
  59.4 1.0 copy.12
  60.9 0.4 stack.4
  61.5 0.4 fusion.3
  62.1 1.4 copy.14
  63.6 5.3 %convolution_convert_fusion.2 = bf16[8,64,4096]{2,1,0:T(8,128)(2,1)S(1)} fusion(bf16[8,128,4096]{2,1,0:T(8,128)(2,1)} %get-tuple-element.8, f32[32,128]{1,0:T(8,128)S(1)} %convolution_select_fusion, f32[64]{0:T(128)S(1)} %iota_convert_fusion), kind=kOutput, calls=%fused_computation.2 | convolution fusion | flops 539230208 | bytes 12599552 | tf_op jit(solution)/shard_map/sct,sth->sch/dot_general | solution.py:403
  69.0 10.3 %multiply_convert_fusion = bf16[512,1024]{1,0:T(8,128)(2,1)S(1)} fusion(bf16[512,4096]{1,0:T(8,128)(2,1)S(1)} %bitcast.40, bf16[4096,1024]{1,0:T(8,128)(2,1)} %param.10, f32[1024]{0:T(1024)S(1)} %get-tuple-element.59, f32[512]{0:T(512)S(1)} %bitcast.47, f32[1024]{0:T(1024)S(1)} %get-tuple-element.58, f32[512]{0:T(512)S(1)} %bitcast.50, f32[512]{0:T(512)S(1)} %bitcast.46, ...), kind=kOutput, calls=%fused_computation.7 | convolution fusion | flops 4304404480 | bytes 13651968 | tf_op jit(solution)/shard_map/dot_general | solution.py:405
  79.3 0.8 select_select_fusion.2
  80.0 0.8 select_select_fusion.1
  80.8 0.8 select_select_fusion
  81.6 0.8 pad_maximum_fusion.refs_1_
  82.4 5.0 %convolution_convert_fusion.1 = bf16[512,4096]{1,0:T(8,128)(2,1)S(1)} fusion(bf16[512,1024]{1,0:T(8,128)(2,1)S(1)} %multiply_convert_fusion, bf16[4096,1024]{1,0:T(8,128)(2,1)S(1)} %bitcast.54), kind=kOutput, calls=%fused_computation.1 | convolution fusion | flops 4297064448 | bytes 13631488 | tf_op jit(solution)/shard_map/dot_general | solution.py:428
  87.4 5.7 %convolution_convert_fusion.refs_0_ = bf16[8,128,4096]{2,1,0:T(8,128)(2,1)} fusion(bf16[8,64,4096]{2,1,0:T(8,128)(2,1)S(1)} %bitcast.55, f32[32,128]{1,0:T(8,128)S(1)} %convolution_select_fusion, f32[64]{0:T(128)S(1)} %iota_convert_fusion), kind=kOutput, calls=%fused_computation | convolution fusion | flops 541327360 | bytes 12599552 | tf_op jit(solution)/shard_map/sct,sch->sth/dot_general | solution.py:431
  93.1 46.1 %back_sum.1 = (bf16[128,4096]{1,0:T(8,128)(2,1)}, bf16[4,512,384]{2,1,0:T(8,128)(2,1)}) custom-call(bf16[8,128,4096]{2,1,0:T(8,128)(2,1)} %convolution_convert_fusion.refs_0_, bf16[512,384]{1,0:T(8,128)(2,1)} %pad_maximum_fusion.refs_1_), custom_call_target="tpu_custom_call" | custom-call | tf_op jit(solution)/shard_map/back_sum/pallas_call | solution.py:228
  139.2 2.3 %constant_dynamic-slice_fusion.own_ref = bf16[512,1024]{1,0:T(8,128)(2,1)} fusion(bf16[512,4096]{1,0:T(8,128)(2,1)} %bitcast.41, s32[]{:T(128)S(6)} %select_n.223), kind=kLoop, calls=%fused_computation.91 | loop fusion | bytes 2097156 | tf_op jit(solution)/shard_map/dynamic_slice | solution.py:441
  141.7 0.9 slice_convert_fusion.pick_ref
  142.6 16.5 %weight_product.1 = bf16[1024,1024]{1,0:T(8,128)(2,1)} custom-call(bf16[512,1024]{1,0:T(8,128)(2,1)} %constant_dynamic-slice_fusion.own_ref, bf16[24,64,128]{2,1,0:T(8,128)(2,1)} %slice_convert_fusion.pick_ref, bf16[3,8,128,1024]{3,2,1,0:T(8,128)(2,1)} %bitcast.37, bf16[4,512,384]{2,1,0:T(8,128)(2,1)} %get-tuple-element.11.packed_ref, f32[2048,3]{1,0:T(8,128)} %bitcast.38), custom_call_target="tpu_custom_call" | custom-call | tf_op jit(solution)/shard_map/weight_product/pallas_call | solution.py:299
  159.1 1.0 copy.16
  (29 shorter events, 1.3 us)
Async XLA Ops:
  7.2 135.4 %all-gather.3.cloned.1.call-start = ((), (), s32[]{:S(2)}) async-start(), calls=%async_computation | async-start | bytes 7077888 | tf_op jit(solution)/shard_map/all_gather | solution.py:367
  69.0 10.3 %copy-start.1 = (bf16[8,64,4096]{2,1,0:T(8,128)(2,1)}, bf16[8,64,4096]{2,1,0:T(8,128)(2,1)S(1)}, u32[]{:S(2)}) copy-start(bf16[8,64,4096]{2,1,0:T(8,128)(2,1)S(1)} %convolution_convert_fusion.2) | copy-start | bytes 12582916
  69.0 13.4 %slice-start = ((s8[8388608]{0:T(1024)(128)(4,1)}), s8[4194304]{0:T(1024)(128)(4,1)S(1)}, s32[]{:S(2)}) async-start(s8[8388608]{0:T(1024)(128)(4,1)} %bitcast.53), calls=%async_computation.1 | async-start | bytes 8388608
  69.0 13.4 %slice-start.1 = ((s8[8388608]{0:T(1024)(128)(4,1)}), s8[4194304]{0:T(1024)(128)(4,1)S(1)}, s32[]{:S(2)}) async-start(s8[8388608]{0:T(1024)(128)(4,1)} %bitcast.53), calls=%async_computation.2 | async-start | bytes 8388608
  142.6 16.5 %copy-start = (bf16[128,4096]{1,0:T(8,128)(2,1)S(1)}, bf16[128,4096]{1,0:T(8,128)(2,1)}, u32[]{:S(2)}) copy-start(bf16[128,4096]{1,0:T(8,128)(2,1)} %get-tuple-element.66) | copy-start | bytes 3145732
Sparse Core Ops, SparseCore 0:
  59.5 44.5 all-gather.2
